TPU v7x, 128 devices: a whole 4x4x4 slice. The times are simulated.
128 devices in a mesh: dp: 2 (over z_hi), seq: 32 (over y, x, core), tensor: 2 (over z_lo).
Axes of the slice: x: 4, y: 4, z: 4 (z_hi: 2, z_lo: 2; z = z_hi * 2 + z_lo), core: 2. Of those that a mesh axis runs over, the one named last changes fastest.
Arguments:
- queries: bfloat16 [2, 16384, 4096], P('dp', 'seq', 'tensor'), may hold values from -6 to 6
- keys: bfloat16 [2, 16384, 4096], P('dp', 'seq', 'tensor'), may hold values from -6 to 6
- values: bfloat16 [2, 16384, 4096], P('dp', 'seq', 'tensor'), may hold values from -40 to 40
- grad_out: bfloat16 [2, 16384, 4096], P('dp', 'seq', 'tensor'), may hold values from -48 to 48
- doc_lengths: int32 [2, 16], P('dp'), may hold values from 1 to 9216, 16384 in all within a row
- gain: float32 [4096], P('tensor'), may hold values from 0.1 to 1.9
Outputs:
- layer_out: bfloat16 [2, 16384, 4096], P('dp', 'seq', 'tensor')
- grad_queries: bfloat16 [2, 16384, 4096], P('dp', 'seq', 'tensor')
- grad_keys: bfloat16 [2, 16384, 4096], P('dp', 'seq', 'tensor')
- grad_values: bfloat16 [2, 16384, 4096], P('dp', 'seq', 'tensor')
- grad_gain: float32 [4096], P('tensor')
Inputs may be any that keep to these rules, and one draw needn't show every extreme that they name: `doc_lengths`: each row sums to 16384; in every sequence the longest document has exactly 9216 tokens.
All inputs are finite; a program needn't handle non-finite values.
Results may differ from a plain program's by a relative error of at most 0.0063.
Values may be sent and summed in bfloat16 or wider, within the bound.
No kernel may reach another device: no remote copies, remote signals or barrier semaphores. Data moves between devices by JAX's collectives and lax.ppermute only.
A program may use at most 128 MiB of HBM per device.

v0:
```python
import jax
import jax.numpy as jnp
from jax import lax
from jax.sharding import PartitionSpec as P

HEADS = 32
HD = 128
epsilon = 1e-05


def prefix(value, axis, join, neutral, backward):
    count = lax.axis_size(axis)
    place = lax.axis_index(axis)
    ahead = count - 1 - place if backward else place
    gathered = jax.tree.map(
        lambda a, kind: lax.all_gather(a.astype(kind), axis), value, (jnp.bfloat16, jnp.bfloat16)
    )
    state = jax.tree.map(lambda a, e: jnp.zeros_like(a) + jnp.asarray(e, a.dtype), value, neutral)

    def one(step, state):
        source = count - 1 - step if backward else step
        return join(
            state,
            jax.tree.map(
                lambda a, own: lax.dynamic_index_in_dim(a, source, 0, False).astype(own.dtype),
                gathered,
                value,
            ),
        )

    return lax.fori_loop(0, ahead, one, state)


def linked(earlier, later):
    keeping = 1.0 - later[1][0]
    return (later[0] + keeping * earlier[0], jnp.maximum(earlier[1], later[1]))


def carried(state, flags, backward):
    blank = jnp.zeros(state.shape, jnp.float32)
    total, unused = prefix(
        (state.astype(jnp.float32), flags),
        "seq",
        linked,
        (blank, jnp.zeros((1,), jnp.float32)),
        backward,
    )
    return total


def head_major(array, shape):
    return jnp.transpose(array.reshape(shape), (1, 0, 2))


def body(queries, keys, values, grad_out, doc_lengths, gain):
    count = queries.shape[1]
    local_width = queries.shape[2]
    local_heads = local_width // HD
    shape = (count, local_heads, HD)
    query = head_major(queries[0], shape)
    key = head_major(keys[0], shape)
    value = head_major(values[0], shape)
    lengths = doc_lengths[0]
    starts = jnp.cumsum(lengths) - lengths
    block = lax.axis_index("seq")
    begin = block * count
    position = begin + jnp.arange(count, dtype=jnp.int32)
    document = jnp.sum((starts[None, :] <= position[:, None]).astype(jnp.int32), axis=1) - 1
    first_doc = document[0]
    last_doc = document[-1]
    numbers = jnp.arange(starts.shape[0], dtype=jnp.int32)
    last_end = jnp.sum(jnp.where(numbers == last_doc, starts + lengths, 0))
    last_block = (last_end - 1) // count
    continues = jnp.logical_not(jnp.any(starts == begin))
    starts_here = jnp.any((starts >= begin) & (starts < begin + count))
    flags = starts_here.astype(jnp.float32).reshape(1)
    first_mask = (document == first_doc) & continues
    last_mask = document == last_doc
    indices = jnp.arange(count, dtype=jnp.int32)
    same = (indices[:, None] >= indices[None, :]) & (document[:, None] == document[None, :])
    key_last = jnp.where(last_mask[None, :, None], key, 0)
    value_last = jnp.where(last_mask[None, :, None], value, 0)
    query_first = jnp.where(first_mask[None, :, None], query, 0)
    state = jnp.einsum("htd,hte->hde", key_last, value, preferred_element_type=jnp.float32).astype(
        jnp.bfloat16
    )
    incoming = carried(state, flags, False)
    carry_in = jnp.where(continues, incoming, 0.0).astype(jnp.bfloat16)
    scores = jnp.einsum("htd,hsd->hts", query, key, preferred_element_type=jnp.float32)
    scores = jnp.where(same[None], scores, 0.0).astype(jnp.bfloat16)
    attended = jnp.einsum("hts,hsd->htd", scores, value, preferred_element_type=jnp.float32)
    attended = attended + jnp.einsum(
        "htd,hde->hte", query_first, carry_in, preferred_element_type=jnp.float32
    )
    attended = jnp.transpose(attended, (1, 0, 2)).reshape(count, local_width)
    squares = lax.psum(jnp.sum(attended * attended, axis=1), "tensor")
    rscale = lax.rsqrt(squares / (HEADS * HD) + epsilon)
    unit = attended * rscale[:, None]
    layer_out = (gain * unit).astype(jnp.bfloat16)
    upstream = grad_out[0].astype(jnp.float32)
    scaled = upstream * gain
    inner = lax.psum(jnp.sum(scaled * unit, axis=1), "tensor") / (HEADS * HD)
    grad_gain = lax.psum(jnp.sum(upstream * unit, axis=0), ("dp", "seq"))
    d_att = head_major(
        (rscale[:, None] * (scaled - unit * inner[:, None])).astype(jnp.bfloat16), shape
    )
    d_first = jnp.where(first_mask[None, :, None], d_att, 0)
    back_state = jnp.einsum(
        "htd,hte->hde", query_first, d_att, preferred_element_type=jnp.float32
    ).astype(jnp.bfloat16)
    outgoing = carried(back_state, flags, True)
    carry_back = jnp.where(last_block > block, outgoing, 0.0).astype(jnp.bfloat16)
    d_scores = jnp.einsum("hte,hse->hts", d_att, value, preferred_element_type=jnp.float32)
    d_scores = jnp.where(same[None], d_scores, 0.0).astype(jnp.bfloat16)
    grad_query = jnp.einsum("hts,hsd->htd", d_scores, key, preferred_element_type=jnp.float32)
    grad_query = grad_query + jnp.einsum(
        "hte,hde->htd", d_first, carry_in, preferred_element_type=jnp.float32
    )
    grad_key = jnp.einsum("hts,htd->hsd", d_scores, query, preferred_element_type=jnp.float32)
    grad_key = grad_key + jnp.einsum(
        "hse,hde->hsd", value_last, carry_back, preferred_element_type=jnp.float32
    )
    grad_value = jnp.einsum("hts,hte->hse", scores, d_att, preferred_element_type=jnp.float32)
    grad_value = grad_value + jnp.einsum(
        "hsd,hde->hse", key_last, carry_back, preferred_element_type=jnp.float32
    )
    out_shape = (1, count, local_width)

    def token_major(array):
        return jnp.transpose(array.astype(jnp.bfloat16), (1, 0, 2)).reshape(out_shape)

    return (
        layer_out.reshape(out_shape),
        token_major(grad_query),
        token_major(grad_key),
        token_major(grad_value),
        grad_gain,
    )


def solution(mesh):
    in_specs = (
        P("dp", "seq", "tensor"),
        P("dp", "seq", "tensor"),
        P("dp", "seq", "tensor"),
        P("dp", "seq", "tensor"),
        P("dp", None),
        P("tensor"),
    )
    out_specs = (
        P("dp", "seq", "tensor"),
        P("dp", "seq", "tensor"),
        P("dp", "seq", "tensor"),
        P("dp", "seq", "tensor"),
        P("tensor"),
    )
    return jax.shard_map(body, mesh=mesh, in_specs=in_specs, out_specs=out_specs, check_vma=False)
```

profile of v0, /device:TPU:0, one launch (start us, length us, event | category | flops | bytes accessed | tf_op | source)
XLA Modules:
  0.0 547.0 jit_solution(15308874766064887949)
XLA Ops:
  8.8 1.3 and_reduce_fusion
  11.5 3.9 copy.79
  15.4 2.9 copy.82
  18.3 1.4 broadcast_compare_fusion
  19.6 3.1 fusion.16
  24.8 69.2 %all-reduce = bf16[32]{0:T(256)(128)(2,1)S(1)} all-reduce(bf16[32]{0:T(256)(128)(2,1)S(1)} %dynamic-update-slice), channel_id=1, replica_groups=mesh['dp'=2,'seq'=32,'tensor'=2] {'seq'}, use_global_device_ids=true, to_apply=%add | all-reduce | flops 32 | bytes 128
  94.1 2.9 copy.78
  97.0 4.1 copy.87
  101.3 4.2 select_convert_fusion.1
  105.5 3.2 copy-done.1
  108.7 4.8 fusion.40
  113.6 5.0 fusion.7
  118.6 5.0 psum.21
  123.6 5.4 copy.88
  129.0 4.0 fusion.2
  133.0 5.1 psum.22
  138.2 4.3 fusion.8
  142.4 1.3 copy-done.7
  143.8 1.6 fusion.17
  145.4 1.3 fusion.25
  147.3 5.4 copy.86
  152.7 4.8 select_convert_fusion
  157.6 4.8 fusion.41
  162.4 4.3 add_convert_fusion.2
  166.7 3.9 copy.96
  170.6 252.2 %psum.23 = f32[2048]{0:T(1024)} all-reduce(f32[2048]{0:T(1024)S(1)} %get-tuple-element.155), channel_id=1, replica_groups=mesh['dp'=2,'seq'=32,'tensor'=2] {'dp','seq'}, use_global_device_ids=true, to_apply=%region_14.15 | all-reduce | flops 2048 | bytes 16384 | tf_op jit(solution)/shard_map/psum | solution.py:103
  422.8 3.9 multiply_convert_fusion
  426.7 6.7 %fusion.42 = f32[16,512,128]{1,2,0:T(8,128)} fusion(bf16[16,512,128]{1,2,0:T(8,128)(2,1)S(1)} %bitcast.105, bf16[16,512,512]{2,1,0:T(8,128)(2,1)} %copy-done), kind=kOutput, calls=%fused_computation.74 | convolution fusion | flops 1073741824 | bytes 14680064 | tf_op jit(solution)/shard_map/hts,htd->hsd/dot_general | solution.py:119
  433.5 86.6 %while.27 = (s32[]{:T(128)}, f32[16,128,128]{2,1,0:T(8,128)S(1)}, s32[]{:T(128)}, bf16[32,16,128,128]{3,2,1,0:T(8,128)(2,1)}, bf16[32,1]{0,1:T(2,128)(2,1)S(1)},...) while((s32[]{:T(128)}, f32[16,128,128]{2,1,0:T(8,128)S(1)}, s32[]{:T(128)}, ...), condition=%wide.region_12.13_spmd, body=%wide.region_11.12_spmd.sunk | while | flops 786439 | bytes 2621605 | solution.py:31
  434.2 2.1 convert_add_fusion.5
  437.0 2.1 convert_add_fusion.5
  439.8 2.1 convert_add_fusion.5
  442.6 2.1 convert_add_fusion.5
  445.4 2.1 convert_add_fusion.5
  448.1 2.1 convert_add_fusion.5
  450.9 2.1 convert_add_fusion.5
  453.7 2.1 convert_add_fusion.5
  456.5 2.1 convert_add_fusion.5
  459.3 2.1 convert_add_fusion.5
  462.1 2.1 convert_add_fusion.5
  464.9 2.1 convert_add_fusion.5
  467.7 2.1 convert_add_fusion.5
  470.4 2.1 convert_add_fusion.5
  473.2 2.1 convert_add_fusion.5
  476.0 2.1 convert_add_fusion.5
  478.8 2.1 convert_add_fusion.5
  481.6 2.1 convert_add_fusion.5
  484.4 2.1 convert_add_fusion.5
  487.2 2.1 convert_add_fusion.5
  489.9 2.1 convert_add_fusion.5
  492.7 2.1 convert_add_fusion.5
  495.5 2.1 convert_add_fusion.5
  498.3 2.1 convert_add_fusion.5
  501.1 2.1 convert_add_fusion.5
  503.9 2.1 convert_add_fusion.5
  506.7 2.1 convert_add_fusion.5
  509.5 2.1 convert_add_fusion.5
  512.2 2.1 convert_add_fusion.5
  515.0 2.1 convert_add_fusion.5
  517.8 2.1 convert_add_fusion.5
  521.8 6.2 %add_convert_fusion = bf16[16,512,128]{1,2,0:T(8,128)(2,1)} fusion(f32[16,512,128]{1,2,0:T(8,128)S(1)} %fusion.14, bf16[16,512,128]{1,2,0:T(8,128)(2,1)S(1)} %copy-done.9, bf16[16,512,512]{2,1,0:T(8,128)(2,1)} %copy-done.1), kind=kOutput, calls=%fused_computation.18 | convolution fusion | flops 1075838976 | bytes 16777216 | tf_op jit(solution)/shard_map/hts,hte->hse/dot_general | solution.py:123
  528.0 4.1 copy.98
  532.1 4.2 add_convert_fusion.1
  536.3 3.9 copy.97
  (77 shorter events, 26.1 us)
Async XLA Ops:
  7.2 106.3 %all-gather.5.cloned.1.call-start = ((), (), s32[]{:S(2)}) async-start(), calls=%async_computation | async-start | bytes 17301504 | tf_op jit(solution)/shard_map/all_gather | solution.py:16
  18.3 4.5 copy-start.2
  19.6 3.9 copy-start.11
  22.8 410.6 %all-gather.7.cloned.1.call-start = ((), (), s32[]{:S(2)}) async-start(), calls=%async_computation.1 | async-start | bytes 17301504 | tf_op jit(solution)/shard_map/all_gather | solution.py:16
  101.3 7.4 %copy-start.3 = (bf16[1,512,2048]{1,2,0:T(8,128)(2,1)S(1)}, bf16[1,512,2048]{1,2,0:T(8,128)(2,1)}, u32[]{:S(2)}) copy-start(bf16[1,512,2048]{1,2,0:T(8,128)(2,1)} %copy-done.2) | copy-start | bytes 6291460
  105.5 3.2 copy-start.1
  123.6 5.4 copy-start.10
  142.4 1.4 copy-start.7
  152.7 4.8 copy-start.5
  157.6 4.8 copy-start
  157.6 4.8 copy-start.8
  433.5 86.7 %copy-start.6 = (bf16[1,512,2048]{1,2,0:T(8,128)(2,1)S(1)}, bf16[1,512,2048]{1,2,0:T(8,128)(2,1)}, u32[]{:S(2)}) copy-start(bf16[1,512,2048]{1,2,0:T(8,128)(2,1)} %copy.79) | copy-start | bytes 6291460
  520.2 1.6 copy-start.9
  528.0 4.1 copy-start.4
Sparse Core Ops, SparseCore 0:
  22.9 75.2 all-gather.4
  145.5 151.3 all-gather.6
where the time goes:
time: 550 us; the launch traced here: 547 us
  blocking collectives  332 us (60%)
  other arithmetic  103 us (19%)
  matrix products  50.3 us (9%)
  local copies, waits for them, and re-layouts  44.8 us (8%)
  between operations  16.2 us (3%)
    psum x1, blocking collectives, body(): grad_gain = lax.psum(jnp.sum(upstream * unit, axis=0), ('dp', 'seq'))  252 us
    unnamed x1, blocking collectives  69.2 us
    add x31, other arithmetic, linked(): return (later[0] + keeping * earlier[0], jnp.maximum(earlier[1], later[1]))  65.4 us
    unnamed x33, local copies, waits for them, and re-layouts  28.3 us
    sub x31, other arithmetic, linked(): keeping = 1.0 - later[1][0]  20.3 us
  transfers between devices with their start and end apart: 2, of which 0 were waited for; matrix products, arithmetic and copies ran while one was open for 10% of the time, Pallas kernels for 0%

commit v1 on v0

--- a/solution.py
+++ b/solution.py
@@ -100,7 +100,7 @@
     upstream = grad_out[0].astype(jnp.float32)
     scaled = upstream * gain
     inner = lax.psum(jnp.sum(scaled * unit, axis=1), "tensor") / (HEADS * HD)
-    grad_gain = lax.psum(jnp.sum(upstream * unit, axis=0), ("dp", "seq"))
+    grad_gain = lax.psum(lax.psum(jnp.sum(upstream * unit, axis=0), "seq"), "dp")
     d_att = head_major(
         (rscale[:, None] * (scaled - unit * inner[:, None])).astype(jnp.bfloat16), shape
     )

time: 550 us -> 453 us (0.82)
  blocking collectives: 332 us -> 235 us
    psum x1 -> x2, blocking collectives: 252 us -> 156 us  [the longest x1 148 us: body(): lax.psum(jnp.sum(upstream * unit, axis=0), 'seq')]
  transfers between devices with their start and end apart: 2 -> 2, of which waited for: 0 -> 0; matrix products, arithmetic and copies ran while one was open for 10% -> 12% of each run, Pallas kernels for 0% -> 0%
where the time goes in v1:
time: 453 us; the launch traced here: 450 us
  blocking collectives  235 us (52%)
  other arithmetic  103 us (23%)
  matrix products  50.4 us (11%)
  local copies, waits for them, and re-layouts  44.8 us (10%)
  between operations  16.2 us (4%)
    psum x1, blocking collectives, body(): lax.psum(jnp.sum(upstream * unit, axis=0), 'seq')  148 us
    unnamed x1, blocking collectives  69.2 us
    add x31, other arithmetic, linked(): return (later[0] + keeping * earlier[0], jnp.maximum(earlier[1], later[1]))  65.4 us
    unnamed x33, local copies, waits for them, and re-layouts  28.3 us
    sub x31, other arithmetic, linked(): keeping = 1.0 - later[1][0]  20.3 us
    reshape x2, local copies, waits for them, and re-layouts, body(): attended = jnp.transpose(attended, (1, 0, 2)).reshape(count, local_width)  10.8 us
  transfers between devices with their start and end apart: 2, of which 0 were waited for; matrix products, arithmetic and copies ran while one was open for 12% of the time, Pallas kernels for 0%

profile of v1, /device:TPU:0, one launch (start us, length us, event | category | flops | bytes accessed | tf_op | source)
XLA Modules:
  0.0 450.4 jit_solution(10993581413240842437)
XLA Ops:
  11.5 3.9 copy.79
  15.4 2.9 copy.82
  18.3 1.4 broadcast_compare_fusion
  19.6 3.1 fusion.16
  24.8 69.2 %all-reduce = bf16[32]{0:T(256)(128)(2,1)S(1)} all-reduce(bf16[32]{0:T(256)(128)(2,1)S(1)} %dynamic-update-slice), channel_id=1, replica_groups=mesh['dp'=2,'seq'=32,'tensor'=2] {'seq'}, use_global_device_ids=true, to_apply=%add | all-reduce | flops 32 | bytes 128
  94.1 2.9 copy.78
  97.0 4.1 copy.87
  101.3 4.2 select_convert_fusion.1
  105.5 3.2 copy-done.1
  108.7 4.8 %fusion.40 = f32[16,512,128]{1,2,0:T(8,128)} fusion(bf16[16,512,512]{2,1,0:T(8,128)(2,1)S(1)} %select_convert_fusion.1, bf16[16,512,128]{1,2,0:T(8,128)(2,1)S(1)} %bitcast.108), kind=kOutput, calls=%fused_computation.72 | convolution fusion | flops 1073741824 | bytes 14680064 | tf_op jit(solution)/shard_map/hts,hsd->htd/dot_general | solution.py:91
  113.6 5.0 %fusion.7 = (f32[512]{0:T(512)S(1)}, f32[16,512,128]{1,2,0:T(8,128)}) fusion(f32[16,512,128]{1,2,0:T(8,128)} %fusion.40, f32[16,128,128]{2,1,0:T(8,128)S(1)} %get-tuple-element.133, pred[]{:T(512)S(6)} %not.3, bf16[16,512,128]{1,2,0:T(8,128)(2,1)S(1)} %bitcast.103, pred[512]{0:T(512)(128)(4,1)S(1)} %get-tuple-element.180), kind=kOutput, calls=%fused_computation.17 | convolution fusion | flops 272891392 | bytes 11536897 | tf_op jit(solution)/shard_map/htd,hde->hte/dot_general | solution.py:92
  118.6 5.0 %psum.28 = f32[512]{0:T(512)S(1)} all-reduce(f32[512]{0:T(512)S(1)} %get-tuple-element.183), channel_id=1, replica_groups=mesh['dp'=2,'seq'=32,'tensor'=2] {'tensor'}, use_global_device_ids=true, to_apply=%region_7.8 | all-reduce | flops 512 | bytes 4096 | tf_op jit(solution)/shard_map/psum | solution.py:96
  123.6 5.4 %copy.88 = f32[512,2048]{1,0:T(8,128)} copy(f32[512,2048]{0,1:T(8,128)} %bitcast.100) | data formatting | bytes 8388608 | tf_op jit(solution)/shard_map/reshape | solution.py:95
  129.0 4.0 fusion.2
  133.0 5.1 %psum.29 = f32[512]{0:T(512)S(1)} all-reduce(f32[512]{0:T(512)S(1)} %get-tuple-element.156), channel_id=1, replica_groups=mesh['dp'=2,'seq'=32,'tensor'=2] {'tensor'}, use_global_device_ids=true, to_apply=%region_9.10 | all-reduce | flops 512 | bytes 4096 | tf_op jit(solution)/shard_map/psum | solution.py:102
  138.2 4.3 fusion.8
  142.4 1.3 copy-done.7
  143.8 1.6 fusion.17
  145.4 1.3 fusion.25
  147.3 5.4 %copy.86 = f32[1,512,2048]{2,1,0:T(8,128)} copy(f32[1,512,2048]{1,2,0:T(8,128)} %bitcast.101) | data formatting | bytes 8388608 | tf_op jit(solution)/shard_map/reshape | solution.py:95
  152.7 4.8 %select_convert_fusion = bf16[16,512,512]{2,1,0:T(8,128)(2,1)S(1)} fusion(bf16[16,512,128]{1,2,0:T(8,128)(2,1)} %copy-done.7, bf16[16,512,128]{1,2,0:T(8,128)(2,1)} %bitcast.107, pred[512,512]{1,0:T(8,128)(4,1)S(1)} %fusion.24), kind=kOutput, calls=%fused_computation.4 | convolution fusion | flops 1082130432 | bytes 12845056 | tf_op jit(solution)/shard_map/hte,hse->hts/dot_general | solution.py:113
  157.6 4.8 %fusion.41 = f32[16,512,128]{1,2,0:T(8,128)} fusion(bf16[16,512,512]{2,1,0:T(8,128)(2,1)S(1)} %select_convert_fusion, bf16[16,512,128]{1,2,0:T(8,128)(2,1)S(1)} %bitcast.112), kind=kOutput, calls=%fused_computation.73 | convolution fusion | flops 1073741824 | bytes 14680064 | tf_op jit(solution)/shard_map/hts,hsd->htd/dot_general | solution.py:115
  162.4 4.3 add_convert_fusion.2
  166.7 3.9 copy.96
  170.6 148.3 %psum.30 = f32[2048]{0:T(1024)S(1)} all-reduce(f32[2048]{0:T(1024)S(1)} %get-tuple-element.155), channel_id=1, replica_groups=mesh['dp'=2,'seq'=32,'tensor'=2] {'seq'}, use_global_device_ids=true, to_apply=%region_14.15 | all-reduce | flops 2048 | bytes 16384 | tf_op jit(solution)/shard_map/psum | solution.py:103
  318.9 7.2 %psum.31 = f32[2048]{0:T(1024)} all-reduce(f32[2048]{0:T(1024)S(1)} %psum.30), channel_id=1, replica_groups=mesh['dp'=2,'seq'=32,'tensor'=2] {'dp'}, use_global_device_ids=true, to_apply=%region_15.16 | all-reduce | flops 2048 | bytes 16384 | tf_op jit(solution)/shard_map/psum | solution.py:103
  326.1 3.9 multiply_convert_fusion
  330.0 6.7 %fusion.42 = f32[16,512,128]{1,2,0:T(8,128)} fusion(bf16[16,512,128]{1,2,0:T(8,128)(2,1)S(1)} %bitcast.105, bf16[16,512,512]{2,1,0:T(8,128)(2,1)} %copy-done), kind=kOutput, calls=%fused_computation.74 | convolution fusion | flops 1073741824 | bytes 14680064 | tf_op jit(solution)/shard_map/hts,htd->hsd/dot_general | solution.py:119
  336.8 86.6 %while.27 = (s32[]{:T(128)}, f32[16,128,128]{2,1,0:T(8,128)S(1)}, s32[]{:T(128)}, bf16[32,16,128,128]{3,2,1,0:T(8,128)(2,1)}, bf16[32,1]{0,1:T(2,128)(2,1)S(1)},...) while((s32[]{:T(128)}, f32[16,128,128]{2,1,0:T(8,128)S(1)}, s32[]{:T(128)}, ...), condition=%wide.region_12.13_spmd, body=%wide.region_11.12_spmd.sunk | while | flops 786439 | bytes 2621605 | solution.py:31
  337.5 2.1 convert_add_fusion.5
  340.3 2.1 convert_add_fusion.5
  343.1 2.1 convert_add_fusion.5
  345.9 2.1 convert_add_fusion.5
  348.7 2.1 convert_add_fusion.5
  351.5 2.1 convert_add_fusion.5
  354.2 2.1 convert_add_fusion.5
  357.0 2.1 convert_add_fusion.5
  359.8 2.1 convert_add_fusion.5
  362.6 2.1 convert_add_fusion.5
  365.4 2.1 convert_add_fusion.5
  368.2 2.1 convert_add_fusion.5
  371.0 2.1 convert_add_fusion.5
  373.8 2.1 convert_add_fusion.5
  376.5 2.1 convert_add_fusion.5
  379.3 2.1 convert_add_fusion.5
  382.1 2.1 convert_add_fusion.5
  384.9 2.1 convert_add_fusion.5
  387.7 2.1 convert_add_fusion.5
  390.5 2.1 convert_add_fusion.5
  393.3 2.1 convert_add_fusion.5
  396.1 2.1 convert_add_fusion.5
  398.8 2.1 convert_add_fusion.5
  401.6 2.1 convert_add_fusion.5
  404.4 2.1 convert_add_fusion.5
  407.2 2.1 convert_add_fusion.5
  410.0 2.1 convert_add_fusion.5
  412.8 2.1 convert_add_fusion.5
  415.6 2.1 convert_add_fusion.5
  418.4 2.1 convert_add_fusion.5
  421.1 2.1 convert_add_fusion.5
  425.1 6.2 %add_convert_fusion = bf16[16,512,128]{1,2,0:T(8,128)(2,1)} fusion(f32[16,512,128]{1,2,0:T(8,128)S(1)} %fusion.14, bf16[16,512,128]{1,2,0:T(8,128)(2,1)S(1)} %copy-done.9, bf16[16,512,512]{2,1,0:T(8,128)(2,1)} %copy-done.1), kind=kOutput, calls=%fused_computation.18 | convolution fusion | flops 1075838976 | bytes 16777216 | tf_op jit(solution)/shard_map/hts,hte->hse/dot_general | solution.py:123
  431.3 4.1 copy.98
  435.4 4.2 add_convert_fusion.1
  439.6 3.9 copy.97
  (78 shorter events, 27.4 us)
Async XLA Ops:
  7.2 106.3 %all-gather.5.cloned.1.call-start = ((), (), s32[]{:S(2)}) async-start(), calls=%async_computation | async-start | bytes 17301504 | tf_op jit(solution)/shard_map/all_gather | solution.py:16
  18.3 4.5 copy-start.2
  19.6 3.9 copy-start.11
  22.8 314.0 %all-gather.7.cloned.1.call-start = ((), (), s32[]{:S(2)}) async-start(), calls=%async_computation.1 | async-start | bytes 17301504 | tf_op jit(solution)/shard_map/all_gather | solution.py:16
  101.3 7.4 %copy-start.3 = (bf16[1,512,2048]{1,2,0:T(8,128)(2,1)S(1)}, bf16[1,512,2048]{1,2,0:T(8,128)(2,1)}, u32[]{:S(2)}) copy-start(bf16[1,512,2048]{1,2,0:T(8,128)(2,1)} %copy-done.2) | copy-start | bytes 6291460
  105.5 3.2 copy-start.1
  123.6 5.4 %copy-start.10 = (f32[2048]{0:T(1024)S(1)}, f32[2048]{0:T(1024)}, u32[]{:S(2)}) copy-start(f32[2048]{0:T(1024)} %param.15) | copy-start | bytes 24580
  142.4 1.4 copy-start.7
  152.7 4.8 %copy-start.5 = (bf16[1,512,2048]{1,2,0:T(8,128)(2,1)S(1)}, bf16[1,512,2048]{1,2,0:T(8,128)(2,1)}, u32[]{:S(2)}) copy-start(bf16[1,512,2048]{1,2,0:T(8,128)(2,1)} %copy.79) | copy-start | bytes 6291460
  157.6 4.8 %copy-start = (bf16[16,512,512]{2,1,0:T(8,128)(2,1)}, bf16[16,512,512]{2,1,0:T(8,128)(2,1)S(1)}, u32[]{:S(2)}) copy-start(bf16[16,512,512]{2,1,0:T(8,128)(2,1)S(1)} %select_convert_fusion) | copy-start | bytes 25165828
  157.6 4.8 %copy-start.8 = (bf16[16,512,128]{1,2,0:T(8,128)(2,1)S(1)}, bf16[16,512,128]{1,2,0:T(8,128)(2,1)}, u32[]{:S(2)}) copy-start(bf16[16,512,128]{1,2,0:T(8,128)(2,1)} %copy-done.7) | copy-start | bytes 6291460
  336.8 86.7 %copy-start.6 = (bf16[1,512,2048]{1,2,0:T(8,128)(2,1)S(1)}, bf16[1,512,2048]{1,2,0:T(8,128)(2,1)}, u32[]{:S(2)}) copy-start(bf16[1,512,2048]{1,2,0:T(8,128)(2,1)} %copy.79) | copy-start | bytes 6291460
  423.5 1.6 copy-start.9
  431.3 4.1 copy-start.4
Sparse Core Ops, SparseCore 0:
  22.9 75.2 all-gather.4
  145.5 151.4 all-gather.6
